TPU v7x, 32 devices: a whole 2x2x4 slice. The times are simulated.
32 devices in a mesh: team: 2 (over x), blk: 4 (over z), head: 4 (over y, core).
Axes of the slice: x: 2, y: 2, z: 4, core: 2. Of those that a mesh axis runs over, the one named last changes fastest.
Arguments:
- queries: bfloat16 [1024, 8, 8, 128], P('blk', 'head', 'team'), may hold values from -40 to 40
- features: bfloat16 [1024, 8192], P('blk', ('team', 'head')), may hold values from -6 to 6
- adapter_down: bfloat16 [4, 8192, 64], P(None, ('team', 'head')), may hold values from -0.0625 to 0.0625
- adapter_key_up: bfloat16 [4, 64, 8, 128], P(None, None, 'head'), may hold values from -0.75 to 0.75
- adapter_value_up: bfloat16 [4, 64, 8, 128], P(None, None, 'head'), may hold values from -0.75 to 0.75
- base_key: bfloat16 [1024, 8, 128], P('blk', 'head'), may hold values from -6 to 6
- base_value: bfloat16 [1024, 8, 128], P('blk', 'head'), may hold values from -24 to 24
- prefix_key: bfloat16 [2048, 8, 128], P('blk', 'head'), may hold values from -7 to 7
- prefix_value: bfloat16 [2048, 8, 128], P('blk', 'head'), may hold values from -24 to 24
- adapter_ids: int32 [4], replicated, may hold values from 0 to 3
- block_order: int32 [4], replicated, may hold values from 0 to 15
Outputs:
- attended: bfloat16 [1024, 8, 8, 128], P('blk', 'head', 'team')
All inputs are finite; a program needn't handle non-finite values.
Results may differ from a plain program's by a relative error of at most 0.011.
Values may be sent and summed in bfloat16 or wider, within the bound.
No kernel may reach another device: no remote copies, remote signals or barrier semaphores. Data moves between devices by JAX's collectives and lax.ppermute only.
A program may use at most 64 MiB of HBM per device.

v0:
```python
import math
import jax
import jax.numpy as jnp
from jax import lax
from jax.sharding import PartitionSpec as P

NEG_FILL = -1e30


def block_length(row_count):
    for candidate in range(min(row_count, 1024), 0, -1):
        if row_count % candidate == 0:
            return candidate
    return row_count


def key_positions(row_count, shard_rows, prefix_dev, query_dev, block_order, block_count):
    row_index = jnp.arange(row_count, dtype=jnp.int32)
    holder = row_index // shard_rows
    within = row_index - holder * shard_rows
    block_ids = jnp.arange(block_count, dtype=jnp.int32)
    holder_order = jnp.sum(
        jnp.where(holder[:, None] == block_ids[None, :], block_order[None, :], 0), axis=1
    )
    later = prefix_dev * block_count + holder_order * query_dev + within - prefix_dev
    return jnp.where(within < prefix_dev, holder * prefix_dev + within, later)


def attend(running, query_rows, query_pos, key_rows, value_rows, key_pos):
    row_count = key_rows.shape[0]
    block_rows = block_length(row_count)
    key_blocks = row_count // block_rows
    kv_heads = key_rows.shape[1]
    head_dim = key_rows.shape[2]
    score_scale = 1.0 / math.sqrt(head_dim)
    latest = jnp.max(query_pos)
    key_split = key_rows.reshape((key_blocks, block_rows, kv_heads, head_dim))
    value_split = value_rows.reshape((key_blocks, block_rows, kv_heads, head_dim))
    pos_split = key_pos.reshape((key_blocks, block_rows))

    def advance(carried, block_data):
        block_keys, block_values, block_pos = block_data

        def compute(previous):
            row_max, row_sum, weighted = previous
            scores = (
                jnp.einsum(
                    "tkgd,skd->kgts", query_rows, block_keys, preferred_element_type=jnp.float32
                )
                * score_scale
            )
            visible = block_pos[None, None, None, :] <= query_pos[None, None, :, None]
            scores = jnp.where(visible, scores, NEG_FILL)
            new_max = jnp.maximum(row_max, jnp.max(scores, axis=-1))
            weights = jnp.where(visible, jnp.exp(scores - new_max[..., None]), 0.0)
            factor = jnp.exp(row_max - new_max)
            row_sum = row_sum * factor + jnp.sum(weights, axis=-1)
            product = jnp.einsum(
                "kgts,skd->kgtd",
                weights.astype(jnp.bfloat16),
                block_values,
                preferred_element_type=jnp.float32,
            )
            weighted = weighted * factor[..., None] + product
            return (new_max, row_sum, weighted)

        return (lax.cond(jnp.min(block_pos) > latest, lambda kept: kept, compute, carried), None)

    result, _ = lax.scan(advance, running, (key_split, value_split, pos_split))
    return result


def on_device(
    queries,
    features,
    adapter_down,
    adapter_key_up,
    adapter_value_up,
    base_key,
    base_value,
    prefix_key,
    prefix_value,
    adapter_ids,
    block_order,
):
    block_count = lax.axis_size("blk")
    my_block = lax.axis_index("blk")
    query_dev = queries.shape[0]
    kv_heads = queries.shape[1]
    group_dev = queries.shape[2]
    head_dim = queries.shape[3]
    prefix_dev = prefix_key.shape[0]
    rank_width = adapter_down.shape[2]
    shard_rows = prefix_dev + query_dev
    chosen = adapter_ids[my_block]
    down_rows = lax.dynamic_index_in_dim(adapter_down, chosen, 0, keepdims=False)
    partial_latent = jnp.dot(features, down_rows, preferred_element_type=jnp.float32)
    latent = lax.psum(partial_latent, ("team", "head")).astype(jnp.bfloat16)

    def expand(up_table, base_rows):
        up_rows = lax.dynamic_index_in_dim(up_table, chosen, 0, keepdims=False).reshape(
            rank_width, kv_heads * head_dim
        )
        delta = jnp.dot(latent, up_rows, preferred_element_type=jnp.float32).reshape(
            query_dev, kv_heads, head_dim
        )
        return (base_rows.astype(jnp.float32) + delta).astype(jnp.bfloat16)

    key_rows = jnp.concatenate([prefix_key, expand(adapter_key_up, base_key)], axis=0)
    value_rows = jnp.concatenate([prefix_value, expand(adapter_value_up, base_value)], axis=0)
    prefix_total = prefix_dev * block_count
    offsets = jnp.arange(query_dev, dtype=jnp.int32)
    query_pos = prefix_total + block_order[my_block] * query_dev + offsets
    initial = (
        jnp.full((kv_heads, group_dev, query_dev), NEG_FILL, jnp.float32),
        jnp.zeros((kv_heads, group_dev, query_dev), jnp.float32),
        jnp.zeros((kv_heads, group_dev, query_dev, head_dim), jnp.float32),
    )
    key_piece = lax.all_gather(key_rows, "blk", axis=0, tiled=True)
    value_piece = lax.all_gather(value_rows, "blk", axis=0, tiled=True)
    piece_pos = key_positions(
        key_piece.shape[0], shard_rows, prefix_dev, query_dev, block_order, block_count
    )
    row_max, row_sum, weighted = attend(
        initial, queries, query_pos, key_piece, value_piece, piece_pos
    )
    result = weighted / row_sum[..., None]
    return result.transpose(2, 0, 1, 3).astype(jnp.bfloat16)


def solution(mesh):
    placed = (
        P("blk", "head", "team", None),
        P("blk", ("team", "head")),
        P(None, ("team", "head"), None),
        P(None, None, "head", None),
        P(None, None, "head", None),
        P("blk", "head", None),
        P("blk", "head", None),
        P("blk", "head", None),
        P("blk", "head", None),
        P(),
        P(),
    )
    return jax.shard_map(
        on_device,
        mesh=mesh,
        in_specs=placed,
        out_specs=P("blk", "head", "team", None),
        check_vma=False,
    )
```

profile of v0, /device:TPU:0, one launch (start us, length us, event | category | flops | bytes accessed | tf_op | source)
XLA Modules:
  0.0 160.4 jit_solution(10820601032562232662)
XLA Ops:
  6.5 1.3 dynamic_slice.39
  9.8 1.2 convolution_bitcast_fusion
  11.0 26.0 %psum.7 = bf16[256,64]{0,1:T(8,128)(2,1)S(1)} all-reduce(f32[256,64]{0,1:T(8,128)S(1)} %convolution_bitcast_fusion), channel_id=1, replica_groups=mesh['team'=2,'blk'=4,'head'=4] {'team','head'}, use_global_device_ids=true, to_apply=%region_0.1 | all-reduce | flops 16384 | bytes 98304 | tf_op jit(solution)/shard_map/psum | solution.py:98
  37.0 1.0 copy.35
  38.0 0.8 constant_dynamic-slice_fusion.1
  38.8 1.1 fusion.21
  39.9 0.8 pad_maximum_fusion
  40.7 0.0 all-gather.3.cloned.1.call-update
  40.7 0.0 all-gather.5.cloned.1.call-start
  40.8 1.0 copy.38
  41.8 1.1 fusion.22
  42.9 0.8 pad_maximum_fusion.1
  43.6 0.0 all-gather.5.cloned.1.call-update
  43.7 1.2 dynamic_slice.38
  45.5 0.6 add_reduce_fusion
  46.1 1.1 copy.40
  47.2 0.8 select_reduce_fusion
  48.1 29.3 %all-gather.3.cloned.1.call-done = bf16[3072,2,128]{2,0,1:T(8,128)(2,1)} async-done(((bf16[768,2,128]{2,0,1:T(8,128)(2,1)}), bf16[3072,2,128]{2,0,1:T(8,128)(2,1)}) %all-gather.3.cloned.1.call-update) | async-done | bytes 1572880 | tf_op jit(solution)/shard_map/all_gather | solution.py:119
  77.4 1.5 copy.39
  78.9 36.0 %all-gather.5.cloned.1.call-done = bf16[3072,2,128]{2,0,1:T(8,128)(2,1)} async-done(((bf16[768,2,128]{2,0,1:T(8,128)(2,1)}), bf16[3072,2,128]{2,0,1:T(8,128)(2,1)}) %all-gather.5.cloned.1.call-update) | async-done | bytes 1572880 | tf_op jit(solution)/shard_map/all_gather | solution.py:120
  114.9 2.7 %copy.41 = bf16[3,1024,2,128]{3,1,2,0:T(8,128)(2,1)} copy(bf16[3,1024,2,128]{3,1,0,2:T(8,128)(2,1)} %bitcast.83) | data formatting | bytes 3145728
  117.6 1.0 broadcast_in_dim.56
  118.6 31.8 %while.15 = (s32[]{:T(128)}, f32[2,4,256]{2,1,0:T(4,128)S(1)}, f32[2,4,256]{2,1,0:T(4,128)S(1)}, f32[2,4,256,128]{3,2,1,0:T(8,128)}, s32[3,1024]{1,0:T(4,128)S(1...) while((s32[]{:T(128)}, f32[2,4,256]{2,1,0:T(4,128)S(1)}, ...), condition=%wide.region_9.10_spmd.clone, body=%wide.region_3.9_spmd.clone.sunk | while | flops 1101796608 | bytes 38421312 | solution.py:69
  118.6 0.6 fusion.45
  120.5 8.7 %conditional.3 = (f32[2,4,256]{2,1,0:T(4,128)S(1)}, f32[2,4,256]{2,1,0:T(4,128)S(1)}, f32[2,4,256,128]{3,2,1,0:T(8,128)}) conditional(s32[]{:T(128)} %convert_element_type.57, (s32[1,1024]{1,0:T(1,128)S(1)}, s32[]{:T(128)}, bf16[3,1024,2,128]{3,1,2,0:T(8,128)(2,1)S(1)}, s32[]{:T(128)}, bf16[256,2,4,128]{3,0,2,1:T(8,128)(2,1)S(1)}, ...), branch_computations={%region_5.7_spmd, %region_8.8_spmd} | conditional | flops 1101795584 | bytes 38395480 | solution.py:67
  120.5 0.2 broadcast_compare_fusion
  120.7 0.0 copy-start.1
  120.7 1.4 fusion.2
  122.2 2.0 %fusion.4 = f32[2,4,256]{2,1,0:T(4,128)S(1)} fusion(f32[2,1024,256,4]{2,1,3,0:T(8,128)S(1)} %get-tuple-element.228, f32[2,4,256]{2,1,0:T(4,128)S(1)} %max.4, pred[256,1024]{0,1:T(8,128)(4,1)S(1)} %broadcast_compare_fusion), kind=kLoop, calls=%fused_computation.5 | loop fusion | flops 10483712 | bytes 8667136 | tf_op jit(solution)/shard_map/while/body/eval_jaxpr/cond/branch_0_fun/reduce_sum | solution.py:57
  124.2 4.0 %fusion.8 = f32[2,4,256,128]{3,2,1,0:T(8,128)S(1)} fusion(f32[2,1024,256,4]{2,1,3,0:T(8,128)S(1)} %get-tuple-element.228, f32[2,4,256]{2,1,0:T(4,128)S(1)} %max.4, pred[256,1024]{0,1:T(8,128)(4,1)S(1)} %broadcast_compare_fusion, f32[2,4,256,128]{3,2,1,0:T(8,128)S(1)} %copy-done.1, bf16[3,1024,2,128]{3,1,2,0:T(8,128)(2,1)} %get-tuple-element.125, ...), kind=kOutput, calls=%fused_computation.8 | convolution fusion | flops 547880960 | bytes 11289088 | tf_op jit(solution)/shard_map/while/body/eval_jaxpr/cond/branch_0_fun/kgts,skd->kgtd/dot_general | solution.py:58
  128.3 1.0 copy-done.2
  129.2 0.6 fusion.45
  131.1 8.7 %conditional.3 = (f32[2,4,256]{2,1,0:T(4,128)S(1)}, f32[2,4,256]{2,1,0:T(4,128)S(1)}, f32[2,4,256,128]{3,2,1,0:T(8,128)}) conditional(s32[]{:T(128)} %convert_element_type.57, (s32[1,1024]{1,0:T(1,128)S(1)}, s32[]{:T(128)}, bf16[3,1024,2,128]{3,1,2,0:T(8,128)(2,1)S(1)}, s32[]{:T(128)}, bf16[256,2,4,128]{3,0,2,1:T(8,128)(2,1)S(1)}, ...), branch_computations={%region_5.7_spmd, %region_8.8_spmd} | conditional | flops 1101795584 | bytes 38395480 | solution.py:67
  131.1 0.2 broadcast_compare_fusion
  131.3 0.0 copy-start.1
  131.3 1.4 fusion.2
  132.8 2.0 %fusion.4 = f32[2,4,256]{2,1,0:T(4,128)S(1)} fusion(f32[2,1024,256,4]{2,1,3,0:T(8,128)S(1)} %get-tuple-element.228, f32[2,4,256]{2,1,0:T(4,128)S(1)} %max.4, pred[256,1024]{0,1:T(8,128)(4,1)S(1)} %broadcast_compare_fusion), kind=kLoop, calls=%fused_computation.5 | loop fusion | flops 10483712 | bytes 8667136 | tf_op jit(solution)/shard_map/while/body/eval_jaxpr/cond/branch_0_fun/reduce_sum | solution.py:57
  134.8 4.0 %fusion.8 = f32[2,4,256,128]{3,2,1,0:T(8,128)S(1)} fusion(f32[2,1024,256,4]{2,1,3,0:T(8,128)S(1)} %get-tuple-element.228, f32[2,4,256]{2,1,0:T(4,128)S(1)} %max.4, pred[256,1024]{0,1:T(8,128)(4,1)S(1)} %broadcast_compare_fusion, f32[2,4,256,128]{3,2,1,0:T(8,128)S(1)} %copy-done.1, bf16[3,1024,2,128]{3,1,2,0:T(8,128)(2,1)} %get-tuple-element.125, ...), kind=kOutput, calls=%fused_computation.8 | convolution fusion | flops 547880960 | bytes 11289088 | tf_op jit(solution)/shard_map/while/body/eval_jaxpr/cond/branch_0_fun/kgts,skd->kgtd/dot_general | solution.py:58
  138.9 1.0 copy-done.2
  139.8 0.6 fusion.45
  141.7 8.7 %conditional.3 = (f32[2,4,256]{2,1,0:T(4,128)S(1)}, f32[2,4,256]{2,1,0:T(4,128)S(1)}, f32[2,4,256,128]{3,2,1,0:T(8,128)}) conditional(s32[]{:T(128)} %convert_element_type.57, (s32[1,1024]{1,0:T(1,128)S(1)}, s32[]{:T(128)}, bf16[3,1024,2,128]{3,1,2,0:T(8,128)(2,1)S(1)}, s32[]{:T(128)}, bf16[256,2,4,128]{3,0,2,1:T(8,128)(2,1)S(1)}, ...), branch_computations={%region_5.7_spmd, %region_8.8_spmd} | conditional | flops 1101795584 | bytes 38395480 | solution.py:67
  141.7 0.2 broadcast_compare_fusion
  141.9 1.4 fusion.2
  143.4 2.0 %fusion.4 = f32[2,4,256]{2,1,0:T(4,128)S(1)} fusion(f32[2,1024,256,4]{2,1,3,0:T(8,128)S(1)} %get-tuple-element.228, f32[2,4,256]{2,1,0:T(4,128)S(1)} %max.4, pred[256,1024]{0,1:T(8,128)(4,1)S(1)} %broadcast_compare_fusion), kind=kLoop, calls=%fused_computation.5 | loop fusion | flops 10483712 | bytes 8667136 | tf_op jit(solution)/shard_map/while/body/eval_jaxpr/cond/branch_0_fun/reduce_sum | solution.py:57
  145.4 4.0 %fusion.8 = f32[2,4,256,128]{3,2,1,0:T(8,128)S(1)} fusion(f32[2,1024,256,4]{2,1,3,0:T(8,128)S(1)} %get-tuple-element.228, f32[2,4,256]{2,1,0:T(4,128)S(1)} %max.4, pred[256,1024]{0,1:T(8,128)(4,1)S(1)} %broadcast_compare_fusion, f32[2,4,256,128]{3,2,1,0:T(8,128)S(1)} %copy-done.1, bf16[3,1024,2,128]{3,1,2,0:T(8,128)(2,1)} %get-tuple-element.125, ...), kind=kOutput, calls=%fused_computation.8 | convolution fusion | flops 547880960 | bytes 11289088 | tf_op jit(solution)/shard_map/while/body/eval_jaxpr/cond/branch_0_fun/kgts,skd->kgtd/dot_general | solution.py:58
  149.5 1.0 copy-done.2
  150.4 0.2 copy.42
  150.6 2.9 %fusion.24 = bf16[256,2,4,128]{3,2,1,0:T(4,128)(2,1)} fusion(f32[2,4,256]{1,0,2:T(2,128)S(1)} %copy.42, f32[2,4,256,128]{3,2,1,0:T(8,128)} %get-tuple-element.142), kind=kLoop, calls=%fused_computation.31 | loop fusion | flops 524288 | bytes 1581056 | tf_op jit(solution)/shard_map/convert_element_type | solution.py:128
  (31 shorter events, 0.2 us)
Async XLA Ops:
  6.5 3.2 %copy-start = (bf16[256,1024]{1,0:T(8,128)(2,1)S(1)}, bf16[256,1024]{1,0:T(8,128)(2,1)}, u32[]{:S(2)}) copy-start(bf16[256,1024]{1,0:T(8,128)(2,1)} %param.16) | copy-start | bytes 1572868
  6.5 70.8 %all-gather.3.cloned.1.call-start = ((), (), s32[]{:S(2)}) async-start(), calls=%async_computation | async-start | bytes 1966080 | tf_op jit(solution)/shard_map/all_gather | solution.py:119
  40.7 74.2 %all-gather.5.cloned.1.call-start = ((), (), s32[]{:S(2)}) async-start(), calls=%async_computation.1 | async-start | bytes 1966080 | tf_op jit(solution)/shard_map/all_gather | solution.py:120
  120.7 3.5 %copy-start.1 = (f32[2,4,256,128]{3,2,1,0:T(8,128)S(1)}, f32[2,4,256,128]{3,2,1,0:T(8,128)}, u32[]{:S(2)}) copy-start(f32[2,4,256,128]{3,2,1,0:T(8,128)} %get-tuple-element.124) | copy-start | bytes 3145732 | tf_op jit(solution)/shard_map/while/body/eval_jaxpr/cond
  128.3 1.0 copy-start.2
  131.3 3.5 %copy-start.1 = (f32[2,4,256,128]{3,2,1,0:T(8,128)S(1)}, f32[2,4,256,128]{3,2,1,0:T(8,128)}, u32[]{:S(2)}) copy-start(f32[2,4,256,128]{3,2,1,0:T(8,128)} %get-tuple-element.124) | copy-start | bytes 3145732 | tf_op jit(solution)/shard_map/while/body/eval_jaxpr/cond
  138.9 1.0 copy-start.2
  141.9 3.5 %copy-start.1 = (f32[2,4,256,128]{3,2,1,0:T(8,128)S(1)}, f32[2,4,256,128]{3,2,1,0:T(8,128)}, u32[]{:S(2)}) copy-start(f32[2,4,256,128]{3,2,1,0:T(8,128)} %get-tuple-element.124) | copy-start | bytes 3145732 | tf_op jit(solution)/shard_map/while/body/eval_jaxpr/cond
  149.5 1.0 copy-start.2
Sparse Core Ops, SparseCore 0:
  40.8 36.4 all-gather.2
  78.9 35.9 all-gather.4
where the time goes:
time: 161 us; the launch traced here: 160 us
  waiting for transfers between devices  65.4 us (41%)
  blocking collectives  26 us (16%)
  matrix products  19.7 us (12%)
  between operations  16 us (10%)
  local copies, waits for them, and re-layouts  14.8 us (9%)
  other arithmetic  14.6 us (9%)
  loops' own time  3.9 us (2%)
    all_gather x1, waiting for transfers between devices, on_device(): value_piece = lax.all_gather(value_rows, 'blk', axis=0, tiled=True)  36 us
    all_gather x1, waiting for transfers between devices, on_device(): key_piece = lax.all_gather(key_rows, 'blk', axis=0, tiled=True)  29.3 us
    psum x1, blocking collectives, on_device(): latent = lax.psum(partial_latent, ('team', 'head')).astype(jnp.bfloat16)  26 us
    dot_general x3, matrix products, compute(): jnp.einsum('kgts,skd->kgtd', weights.astype(jnp.bfloat16), block_values,...  12.1 us
    unnamed x7, local copies, waits for them, and re-layouts  7.28 us
    reduce_sum x3, other arithmetic, compute(): row_sum = row_sum * factor + jnp.sum(weights, axis=-1)  6.09 us
    dot_general x3, matrix products, compute(): jnp.einsum('tkgd,skd->kgts', query_rows, block_keys, preferred_element_ty...  4.2 us
    another operation x1, loops' own time, attend(): result, _ = lax.scan(advance, running, (key_split, value_split, pos_split))  3.67 us
  transfers between devices with their start and end apart: 2, of which 2 were waited for; matrix products, arithmetic and copies ran while one was open for 5% of the time, Pallas kernels for 0%

commit v1 on v0

--- a/solution.py
+++ b/solution.py
@@ -5,6 +5,11 @@
 from jax.sharding import PartitionSpec as P
 
 NEG_FILL = -1e30
+run_the_yards = lambda v0, vec, peer_axis: jnp.split(
+    lax.all_gather(jnp.concatenate([v0, vec], 1), peer_axis, axis=0, tiled=True),
+    [v0.shape[1]],
+    axis=1,
+)
 
 
 def block_length(row_count):
@@ -116,8 +121,7 @@
         jnp.zeros((kv_heads, group_dev, query_dev), jnp.float32),
         jnp.zeros((kv_heads, group_dev, query_dev, head_dim), jnp.float32),
     )
-    key_piece = lax.all_gather(key_rows, "blk", axis=0, tiled=True)
-    value_piece = lax.all_gather(value_rows, "blk", axis=0, tiled=True)
+    key_piece, value_piece = run_the_yards(key_rows, value_rows, "blk")
     piece_pos = key_positions(
         key_piece.shape[0], shard_rows, prefix_dev, query_dev, block_order, block_count
     )

time: 161 us -> 153 us (0.950)
  waiting for transfers between devices: 65.4 us -> 58.5 us
    all_gather x2 -> x1, waiting for transfers between devices: 65.3 us -> 58.5 us  [lax.all_gather(jnp.concatenate([v0, vec], 1), peer_axis, axis=0, tiled=True)]
    unnamed x7, local copies, waits for them, and re-layouts: 7.28 us -> 4.45 us
    split x0 -> x1, local copies, waits for them, and re-layouts: none -> 2.08 us  [jnp.split(lax.all_gather(jnp.concatenate([v0, vec], 1), peer_axis, axis=0...]
  transfers between devices with their start and end apart: 2 -> 1, of which waited for: 2 -> 1; matrix products, arithmetic and copies ran while one was open for 5% -> 3% of each run, Pallas kernels for 0% -> 0%
where the time goes in v1:
time: 153 us
  waiting for transfers between devices  58.5 us (38%)
  blocking collectives  26 us (17%)
  matrix products  19.7 us (13%)
  between operations  16.2 us (11%)
  local copies, waits for them, and re-layouts  14.1 us (9%)
  other arithmetic  14.1 us (9%)
  loops' own time  3.94 us (3%)
    all_gather x1, waiting for transfers between devices, lax.all_gather(jnp.concatenate([v0, vec], 1), peer_axis, axis=0, tiled=True)  58.5 us
    psum x1, blocking collectives, on_device(): latent = lax.psum(partial_latent, ('team', 'head')).astype(jnp.bfloat16)  26 us
    dot_general x3, matrix products, compute(): jnp.einsum('kgts,skd->kgtd', weights.astype(jnp.bfloat16), block_values,...  12.1 us
    reduce_sum x3, other arithmetic, compute(): row_sum = row_sum * factor + jnp.sum(weights, axis=-1)  6.09 us
    unnamed x7, local copies, waits for them, and re-layouts  4.45 us
    dot_general x3, matrix products, compute(): jnp.einsum('tkgd,skd->kgts', query_rows, block_keys, preferred_element_ty...  4.2 us
    another operation x1, loops' own time, attend(): result, _ = lax.scan(advance, running, (key_split, value_split, pos_split))  3.7 us
  transfers between devices with their start and end apart: 1, of which 1 were waited for; matrix products, arithmetic and copies ran while one was open for 3% of the time, Pallas kernels for 0%

profile of v1, /device:TPU:0, one launch (start us, length us, event | category | flops | bytes accessed | tf_op | source)
XLA Modules:
  0.0 152.6 jit_solution(7637905259982797117)
XLA Ops:
  6.5 0.0 copy-start
  6.5 1.4 dynamic_slice.39
  10.0 1.2 convolution_bitcast_fusion
  11.2 26.0 %psum.7 = bf16[256,64]{0,1:T(8,128)(2,1)S(1)} all-reduce(f32[256,64]{0,1:T(8,128)S(1)} %convolution_bitcast_fusion), channel_id=1, replica_groups=mesh['team'=2,'blk'=4,'head'=4] {'team','head'}, use_global_device_ids=true, to_apply=%region_0.1 | all-reduce | flops 16384 | bytes 98304 | tf_op jit(solution)/shard_map/psum | solution.py:103
  37.2 1.0 copy.35
  38.2 1.0 copy.38
  39.2 0.8 constant_dynamic-slice_fusion.1
  40.0 1.1 fusion.21
  41.1 1.1 fusion.22
  42.2 0.9 maximum_maximum_fusion
  43.2 0.0 all-gather.2.cloned.1.call-update
  43.2 1.3 dynamic_slice.38
  45.1 0.7 add_reduce_fusion
  45.8 1.1 copy.40
  46.9 0.8 select_reduce_fusion
  47.7 58.5 %all-gather.2.cloned.1.call-done = bf16[3072,4,128]{2,0,1:T(8,128)(2,1)} async-done(((bf16[768,4,128]{2,0,1:T(8,128)(2,1)}), bf16[3072,4,128]{2,0,1:T(8,128)(2,1)}) %all-gather.2.cloned.1.call-update) | async-done | bytes 3145744 | tf_op jit(solution)/shard_map/all_gather | solution.py:9
  106.2 2.1 %fusion.42 = (bf16[3072,2,128]{2,0,1:T(8,128)(2,1)S(1)}, bf16[3072,2,128]{2,0,1:T(8,128)(2,1)S(1)}) fusion(bf16[3072,4,128]{2,0,1:T(8,128)(2,1)} %all-gather.2.cloned.1.call-done), kind=kLoop, calls=%fused_computation.68 | loop fusion | bytes 6291456 | tf_op jit(solution)/shard_map/split | solution.py:8
  108.3 0.1 copy.39
  108.4 1.3 copy.41
  109.7 1.0 broadcast_in_dim.56
  110.7 31.9 %while.15 = (s32[]{:T(128)}, f32[2,4,256]{2,1,0:T(4,128)S(1)}, f32[2,4,256]{2,1,0:T(4,128)S(1)}, f32[2,4,256,128]{3,2,1,0:T(8,128)}, s32[3,1024]{1,0:T(4,128)S(1...) while((s32[]{:T(128)}, f32[2,4,256]{2,1,0:T(4,128)S(1)}, ...), condition=%wide.region_9.10_spmd.clone, body=%wide.region_3.9_spmd.clone.sunk | while | flops 1101796608 | bytes 38421312 | solution.py:74
  110.7 0.7 fusion.46
  112.6 8.7 %conditional.3 = (f32[2,4,256]{2,1,0:T(4,128)S(1)}, f32[2,4,256]{2,1,0:T(4,128)S(1)}, f32[2,4,256,128]{3,2,1,0:T(8,128)}) conditional(s32[]{:T(128)} %convert_element_type.57, (s32[1,1024]{1,0:T(1,128)S(1)}, s32[]{:T(128)}, bf16[3,1024,2,128]{3,1,2,0:T(8,128)(2,1)S(1)}, s32[]{:T(128)}, bf16[256,2,4,128]{3,0,2,1:T(8,128)(2,1)S(1)}, ...), branch_computations={%region_5.7_spmd, %region_8.8_spmd} | conditional | flops 1101795584 | bytes 38395480 | solution.py:72
  112.6 0.2 broadcast_compare_fusion
  112.8 0.0 copy-start.1
  112.8 1.4 fusion.2
  114.3 2.0 %fusion.4 = f32[2,4,256]{2,1,0:T(4,128)S(1)} fusion(f32[2,1024,256,4]{2,1,3,0:T(8,128)S(1)} %get-tuple-element.228, f32[2,4,256]{2,1,0:T(4,128)S(1)} %max.4, pred[256,1024]{0,1:T(8,128)(4,1)S(1)} %broadcast_compare_fusion), kind=kLoop, calls=%fused_computation.5 | loop fusion | flops 10483712 | bytes 8667136 | tf_op jit(solution)/shard_map/while/body/eval_jaxpr/cond/branch_0_fun/reduce_sum | solution.py:62
  116.3 4.0 %fusion.8 = f32[2,4,256,128]{3,2,1,0:T(8,128)S(1)} fusion(f32[2,1024,256,4]{2,1,3,0:T(8,128)S(1)} %get-tuple-element.228, f32[2,4,256]{2,1,0:T(4,128)S(1)} %max.4, pred[256,1024]{0,1:T(8,128)(4,1)S(1)} %broadcast_compare_fusion, f32[2,4,256,128]{3,2,1,0:T(8,128)S(1)} %copy-done.1, bf16[3,1024,2,128]{3,1,2,0:T(8,128)(2,1)} %get-tuple-element.125, ...), kind=kOutput, calls=%fused_computation.8 | convolution fusion | flops 547880960 | bytes 11289088 | tf_op jit(solution)/shard_map/while/body/eval_jaxpr/cond/branch_0_fun/kgts,skd->kgtd/dot_general | solution.py:63
  120.4 1.0 copy-done.2
  121.3 0.7 fusion.46
  123.2 8.7 %conditional.3 = (f32[2,4,256]{2,1,0:T(4,128)S(1)}, f32[2,4,256]{2,1,0:T(4,128)S(1)}, f32[2,4,256,128]{3,2,1,0:T(8,128)}) conditional(s32[]{:T(128)} %convert_element_type.57, (s32[1,1024]{1,0:T(1,128)S(1)}, s32[]{:T(128)}, bf16[3,1024,2,128]{3,1,2,0:T(8,128)(2,1)S(1)}, s32[]{:T(128)}, bf16[256,2,4,128]{3,0,2,1:T(8,128)(2,1)S(1)}, ...), branch_computations={%region_5.7_spmd, %region_8.8_spmd} | conditional | flops 1101795584 | bytes 38395480 | solution.py:72
  123.2 0.2 broadcast_compare_fusion
  123.5 0.0 copy-start.1
  123.5 1.4 fusion.2
  124.9 2.0 %fusion.4 = f32[2,4,256]{2,1,0:T(4,128)S(1)} fusion(f32[2,1024,256,4]{2,1,3,0:T(8,128)S(1)} %get-tuple-element.228, f32[2,4,256]{2,1,0:T(4,128)S(1)} %max.4, pred[256,1024]{0,1:T(8,128)(4,1)S(1)} %broadcast_compare_fusion), kind=kLoop, calls=%fused_computation.5 | loop fusion | flops 10483712 | bytes 8667136 | tf_op jit(solution)/shard_map/while/body/eval_jaxpr/cond/branch_0_fun/reduce_sum | solution.py:62
  127.0 4.0 %fusion.8 = f32[2,4,256,128]{3,2,1,0:T(8,128)S(1)} fusion(f32[2,1024,256,4]{2,1,3,0:T(8,128)S(1)} %get-tuple-element.228, f32[2,4,256]{2,1,0:T(4,128)S(1)} %max.4, pred[256,1024]{0,1:T(8,128)(4,1)S(1)} %broadcast_compare_fusion, f32[2,4,256,128]{3,2,1,0:T(8,128)S(1)} %copy-done.1, bf16[3,1024,2,128]{3,1,2,0:T(8,128)(2,1)} %get-tuple-element.125, ...), kind=kOutput, calls=%fused_computation.8 | convolution fusion | flops 547880960 | bytes 11289088 | tf_op jit(solution)/shard_map/while/body/eval_jaxpr/cond/branch_0_fun/kgts,skd->kgtd/dot_general | solution.py:63
  131.0 1.0 copy-done.2
  132.0 0.7 fusion.46
  133.8 8.7 %conditional.3 = (f32[2,4,256]{2,1,0:T(4,128)S(1)}, f32[2,4,256]{2,1,0:T(4,128)S(1)}, f32[2,4,256,128]{3,2,1,0:T(8,128)}) conditional(s32[]{:T(128)} %convert_element_type.57, (s32[1,1024]{1,0:T(1,128)S(1)}, s32[]{:T(128)}, bf16[3,1024,2,128]{3,1,2,0:T(8,128)(2,1)S(1)}, s32[]{:T(128)}, bf16[256,2,4,128]{3,0,2,1:T(8,128)(2,1)S(1)}, ...), branch_computations={%region_5.7_spmd, %region_8.8_spmd} | conditional | flops 1101795584 | bytes 38395480 | solution.py:72
  133.9 0.2 broadcast_compare_fusion
  134.1 0.0 copy-start.1
  134.1 1.4 fusion.2
  135.5 2.0 %fusion.4 = f32[2,4,256]{2,1,0:T(4,128)S(1)} fusion(f32[2,1024,256,4]{2,1,3,0:T(8,128)S(1)} %get-tuple-element.228, f32[2,4,256]{2,1,0:T(4,128)S(1)} %max.4, pred[256,1024]{0,1:T(8,128)(4,1)S(1)} %broadcast_compare_fusion), kind=kLoop, calls=%fused_computation.5 | loop fusion | flops 10483712 | bytes 8667136 | tf_op jit(solution)/shard_map/while/body/eval_jaxpr/cond/branch_0_fun/reduce_sum | solution.py:62
  137.6 0.0 copy-done.1
  137.6 4.0 %fusion.8 = f32[2,4,256,128]{3,2,1,0:T(8,128)S(1)} fusion(f32[2,1024,256,4]{2,1,3,0:T(8,128)S(1)} %get-tuple-element.228, f32[2,4,256]{2,1,0:T(4,128)S(1)} %max.4, pred[256,1024]{0,1:T(8,128)(4,1)S(1)} %broadcast_compare_fusion, f32[2,4,256,128]{3,2,1,0:T(8,128)S(1)} %copy-done.1, bf16[3,1024,2,128]{3,1,2,0:T(8,128)(2,1)} %get-tuple-element.125, ...), kind=kOutput, calls=%fused_computation.8 | convolution fusion | flops 547880960 | bytes 11289088 | tf_op jit(solution)/shard_map/while/body/eval_jaxpr/cond/branch_0_fun/kgts,skd->kgtd/dot_general | solution.py:63
  141.6 1.0 copy-done.2
  142.6 0.2 copy.42
  142.8 2.9 %fusion.24 = bf16[256,2,4,128]{3,2,1,0:T(4,128)(2,1)} fusion(f32[2,4,256]{1,0,2:T(2,128)S(1)} %copy.42, f32[2,4,256,128]{3,2,1,0:T(8,128)} %get-tuple-element.142), kind=kLoop, calls=%fused_computation.32 | loop fusion | flops 524288 | bytes 1581056 | tf_op jit(solution)/shard_map/convert_element_type | solution.py:132
  (28 shorter events, 0.2 us)
Async XLA Ops:
  6.5 3.5 %copy-start = (bf16[256,1024]{1,0:T(8,128)(2,1)S(1)}, bf16[256,1024]{1,0:T(8,128)(2,1)}, u32[]{:S(2)}) copy-start(bf16[256,1024]{1,0:T(8,128)(2,1)} %param.16) | copy-start | bytes 1572868
  6.5 99.7 %all-gather.2.cloned.1.call-start = ((), (), s32[]{:S(2)}) async-start(), calls=%async_computation | async-start | bytes 3932160 | tf_op jit(solution)/shard_map/all_gather | solution.py:9
  112.8 3.5 %copy-start.1 = (f32[2,4,256,128]{3,2,1,0:T(8,128)S(1)}, f32[2,4,256,128]{3,2,1,0:T(8,128)}, u32[]{:S(2)}) copy-start(f32[2,4,256,128]{3,2,1,0:T(8,128)} %get-tuple-element.124) | copy-start | bytes 3145732 | tf_op jit(solution)/shard_map/while/body/eval_jaxpr/cond
  120.4 1.0 copy-start.2
  123.5 3.5 %copy-start.1 = (f32[2,4,256,128]{3,2,1,0:T(8,128)S(1)}, f32[2,4,256,128]{3,2,1,0:T(8,128)}, u32[]{:S(2)}) copy-start(f32[2,4,256,128]{3,2,1,0:T(8,128)} %get-tuple-element.124) | copy-start | bytes 3145732 | tf_op jit(solution)/shard_map/while/body/eval_jaxpr/cond
  131.0 1.0 copy-start.2
  134.1 3.5 %copy-start.1 = (f32[2,4,256,128]{3,2,1,0:T(8,128)S(1)}, f32[2,4,256,128]{3,2,1,0:T(8,128)}, u32[]{:S(2)}) copy-start(f32[2,4,256,128]{3,2,1,0:T(8,128)} %get-tuple-element.124) | copy-start | bytes 3145732 | tf_op jit(solution)/shard_map/while/body/eval_jaxpr/cond
  141.6 1.0 copy-start.2
Sparse Core Ops, SparseCore 0:
  43.3 62.8 all-gather.1
